TPU v7x, 128 devices: a whole 4x4x4 slice. The times are simulated.
128 devices in a mesh: pop: 8 (over x, core), unit: 16 (over z, y).
Axes of the slice: x: 4, y: 4, z: 4, core: 2. Of those that a mesh axis runs over, the one named last changes fastest.
Arguments:
- states: bfloat16 [4, 4096, 1024], P(None, 'unit', 'pop'), may hold values from -6 to 6
- gate_inputs: bfloat16 [4, 3, 4096, 1024], P(None, None, 'unit', 'pop'), may hold values from -6 to 6
- actions: bfloat16 [4, 128, 1024], P(None, None, 'pop'), may hold values from -0.8984375 to 0.8984375
- final_grad: bfloat16 [4096, 1024], P('unit', 'pop'), may hold values from -6 to 6
- recur_weight: bfloat16 [4096, 3, 4096], P(None, None, 'unit'), may hold values from -0.09375 to 0.09375
- act_weight: bfloat16 [128, 3, 4096], P(None, None, 'unit'), may hold values from -0.5 to 0.5
- opp_first: bfloat16 [32, 4096, 4096], P('pop', None, 'unit'), may hold values from -0.09375 to 0.09375
- opp_second: bfloat16 [32, 128, 4096], P('pop'), may hold values from -0.09375 to 0.09375
- opponent: int32 [1024, 1], P('pop'), may hold values from 0 to 31; in each aligned block of 128 rows (0 to 127, 128 to 255, ...) at most 12 rows name the same one
Outputs:
- start_grad: bfloat16 [4096, 1024], P('unit', 'pop')
- act_weight_grad: float32 [128, 3, 4096], P(None, None, 'unit')
Inputs may be any that keep to these rules, and one draw needn't show every extreme that they name: In each aligned block of 128 rows (the rows of one index of pop) no opponent is named by more than 12 rows, a bound that some block reaches.
All inputs are finite; a program needn't handle non-finite values.
Results may differ from a plain program's by a relative error of at most 0.02.
Values may be sent and summed in bfloat16 or wider, within the bound.
A program may use at most 128 MiB of HBM per device.

v0:
```python
import jax
import jax.numpy as jnp
from jax import lax
from jax.sharding import PartitionSpec as P

CAP = 12


def gru_backward(gradient, pre_gates, latent):
    reset = jax.nn.sigmoid(pre_gates[0].astype(jnp.float32))
    cand_input = pre_gates[1].astype(jnp.float32)
    update = jax.nn.sigmoid(pre_gates[2].astype(jnp.float32) - 1.0)
    candidate = jnp.tanh(reset * cand_input)
    grad_cand = gradient * update * (1.0 - candidate * candidate)
    grad_reset = grad_cand * cand_input * reset * (1.0 - reset)
    grad_input = grad_cand * reset
    grad_update = gradient * (candidate - latent.astype(jnp.float32)) * update * (1.0 - update)
    direct = gradient * (1.0 - update)
    return (direct, jnp.stack([grad_reset, grad_input, grad_update]).astype(jnp.bfloat16))


def silu_slope(values):
    logistic = jax.nn.sigmoid(values)
    return logistic * (1.0 + values * (1.0 - logistic))


def hidden_slope(received, opp_first):
    members_here = received.shape[1]
    partial_sum = jnp.concatenate(
        [
            jnp.dot(opp_first[member], received[:, member, :], preferred_element_type=jnp.float32)
            for member in range(members_here)
        ],
        axis=1,
    )
    summed = lax.psum(partial_sum.astype(jnp.bfloat16), "unit").astype(jnp.float32)
    return silu_slope(summed)


def opponent_backward(slope, incoming, opp_first, opp_second):
    members_here = incoming.shape[1]
    slot_count = incoming.shape[2]
    upward = jnp.concatenate(
        [
            jnp.dot(
                opp_second[member].T, incoming[:, member, :], preferred_element_type=jnp.float32
            )
            for member in range(members_here)
        ],
        axis=1,
    )
    scaled = (upward * slope).astype(jnp.bfloat16)
    backward = jnp.concatenate(
        [
            jnp.dot(
                opp_first[member].T,
                scaled[:, member * slot_count : (member + 1) * slot_count],
                preferred_element_type=jnp.float32,
            )
            for member in range(members_here)
        ],
        axis=1,
    )
    return backward.astype(jnp.bfloat16).reshape(opp_first.shape[2], members_here, slot_count)


def body(
    states,
    gate_inputs,
    actions,
    final_grad,
    recur_weight,
    act_weight,
    opp_first,
    opp_second,
    opponent,
):
    step_count = states.shape[0]
    share = states.shape[1]
    row_count = states.shape[2]
    groups = lax.axis_size("pop")
    members_here = opp_first.shape[0]
    slot_count = groups * CAP
    population = members_here * groups
    chosen = opponent[:, 0]
    onehot = (chosen[:, None] == jnp.arange(population, dtype=jnp.int32)[None, :]).astype(jnp.int32)
    position = jnp.sum((jnp.cumsum(onehot, axis=0) - onehot) * onehot, axis=1)
    column = chosen % members_here * slot_count + chosen // members_here * CAP + position
    packing = (
        column[:, None] == jnp.arange(members_here * slot_count, dtype=jnp.int32)[None, :]
    ).astype(jnp.bfloat16)

    def pack_rows(values):
        packed = jnp.dot(values, packing, preferred_element_type=jnp.float32).astype(jnp.bfloat16)
        return packed.reshape(values.shape[0], members_here, slot_count)

    recur_flat = recur_weight.reshape(recur_weight.shape[0], -1)
    action_flat = act_weight.reshape(act_weight.shape[0], -1)
    gradient = final_grad.astype(jnp.float32)
    weight_grad = jnp.zeros(action_flat.shape, jnp.float32)
    for step in reversed(range(step_count)):
        direct, pre_grads = gru_backward(gradient, gate_inputs[step], states[step])
        flat_grads = pre_grads.reshape(-1, row_count)
        carried = lax.psum_scatter(
            jnp.dot(recur_flat, flat_grads, preferred_element_type=jnp.float32).astype(
                jnp.bfloat16
            ),
            "unit",
            scatter_dimension=0,
            tiled=True,
        ).astype(jnp.float32)
        action_grad = lax.psum(
            jnp.dot(action_flat, flat_grads, preferred_element_type=jnp.float32).astype(
                jnp.bfloat16
            ),
            "unit",
        ).astype(jnp.float32)
        weight_grad = weight_grad + jnp.dot(
            actions[step], flat_grads.T, preferred_element_type=jnp.float32
        )
        taken = actions[step].astype(jnp.float32)
        policy_grad = (action_grad * (1.0 - taken * taken)).astype(jnp.bfloat16)
        packed_grad = pack_rows(policy_grad)
        arrived_state, incoming = (
            lax.all_to_all(pack_rows(states[step]), "pop", split_axis=2, concat_axis=2, tiled=True),
            lax.all_to_all(packed_grad, "pop", split_axis=2, concat_axis=2, tiled=True),
        )
        slope = hidden_slope(arrived_state, opp_first)
        returned = lax.all_to_all(
            opponent_backward(slope, incoming, opp_first, opp_second),
            "pop",
            split_axis=2,
            concat_axis=2,
            tiled=True,
        )
        from_opponent = jnp.dot(
            returned.reshape(share, -1), packing.T, preferred_element_type=jnp.float32
        )
        gradient = direct + carried + from_opponent
    summed_weight = lax.psum(weight_grad.astype(jnp.bfloat16), "pop").astype(jnp.float32)
    return (gradient.astype(jnp.bfloat16), summed_weight.reshape(act_weight.shape))


def solution(mesh):
    placed = (
        P(None, "unit", "pop"),
        P(None, None, "unit", "pop"),
        P(None, None, "pop"),
        P("unit", "pop"),
        P(None, None, "unit"),
        P(None, None, "unit"),
        P("pop", None, "unit"),
        P("pop", None, None),
        P("pop", None),
    )
    return jax.shard_map(
        body,
        mesh=mesh,
        in_specs=placed,
        out_specs=(P("unit", "pop"), P(None, None, "unit")),
        check_vma=False,
    )
```

profile of v0, /device:TPU:0, one launch (start us, length us, event | category | flops | bytes accessed | tf_op | source)
XLA Modules:
  0.0 733.9 jit_solution(13641392170880029019)
XLA Ops:
  11.7 4.4 all-to-all-start.1
  22.9 4.0 all-to-all-start.4
  27.1 2.4 fusion.36
  29.5 2.4 fusion.37
  31.9 2.4 fusion.38
  34.2 2.4 fusion.39
  37.3 4.8 all-to-all-start.7
  42.1 1.6 fusion.381
  43.7 3.2 fusion.40
  47.0 3.3 fusion.41
  50.2 3.3 fusion.42
  53.5 3.3 fusion.43
  56.7 4.8 all-to-all-start.10
  62.2 3.2 fusion.44
  65.4 3.2 fusion.45
  68.7 3.3 fusion.46
  71.9 3.3 fusion.47
  76.8 2.4 fusion.48
  79.2 2.5 fusion.49
  81.7 2.4 fusion.50
  84.1 2.4 fusion.51
  86.5 3.1 pad_maximum_fusion
  90.0 3.0 pad_maximum_fusion.2
  95.4 78.4 %psum.63 = bf16[128,128]{0,1:T(8,128)(2,1)S(1)} all-reduce(bf16[128,128]{0,1:T(8,128)(2,1)S(1)} %fusion.205), channel_id=1, replica_groups=mesh['pop'=8,'unit'=16] {'unit'}, use_global_device_ids=true, to_apply=%region_1.2 | all-reduce | flops 16384 | bytes 65536 | tf_op jit(solution)/shard_map/psum | solution.py:112
  174.9 4.9 all-to-all-start
  180.4 6.1 fusion.35
  197.8 1.7 convolution_bitcast_fusion.16
  204.2 72.7 %all-reduce.6.cloned.1.call-done = (bf16[4096,384]{0,1:T(8,128)(2,1)}, bf16[4096,384]{0,1:T(8,128)(2,1)}, bf16[4096,384]{0,1:T(8,128)(2,1)}, bf16[4096,384]{0,1:T(8,128)(2,1)}) async-done(((bf16[4096,384]{0,1:T(8,128)(2,1)}, bf16[4096,384]{0,1:T(8,128)(2,1)}, bf16[4096,384]{0,1:T(8,128)(2,1)}, bf16[4096,384]{0,1:T(8,128)(2,1)}), (bf16[4096,384]{0,1:T(8,128)(2,1)}, bf16[4096,384]{0,1:T(8,128)(2,1)}, ...) | async-done | bytes 12582928 | tf_op jit(solution)/shard_map/psum | solution.py:36
  276.9 4.4 fusion.6
  281.3 2.1 fusion.163
  283.4 2.1 fusion.175
  285.5 2.1 fusion.187
  287.7 2.1 fusion.199
  290.7 4.3 all-to-all-start.2
  295.2 6.6 all-to-all-done.2
  301.8 51.3 %reduce-scatter.5.cloned.1.call-done = bf16[256,128]{0,1:T(8,128)(2,1)} async-done(((bf16[4096,128]{0,1:T(8,128)(2,1)}), bf16[256,128]{0,1:T(8,128)(2,1)}) %reduce-scatter.5.cloned.1.call-update) | async-done | bytes 65552 | tf_op jit(solution)/shard_map/reduce_scatter | solution.py:104
  354.4 5.9 fusion.34
  360.6 72.2 %psum.65 = bf16[128,128]{0,1:T(8,128)(2,1)S(1)} all-reduce(bf16[128,128]{0,1:T(8,128)(2,1)S(1)} %fusion.204), channel_id=1, replica_groups=mesh['pop'=8,'unit'=16] {'unit'}, use_global_device_ids=true, to_apply=%region_6.7 | all-reduce | flops 16384 | bytes 65536 | tf_op jit(solution)/shard_map/psum | solution.py:112
  433.9 4.5 all-to-all-start.3
  438.6 5.6 all-to-all-done.3
  444.3 1.7 convolution_bitcast_fusion.12
  446.0 1.7 convolution_bitcast_fusion.13
  448.5 2.7 fusion.13
  454.4 3.4 all-to-all-start.5
  458.1 6.5 all-to-all-done.5
  465.9 5.9 fusion.33
  472.1 69.6 %psum.67 = bf16[128,128]{0,1:T(8,128)(2,1)S(1)} all-reduce(bf16[128,128]{0,1:T(8,128)(2,1)S(1)} %fusion.203), channel_id=1, replica_groups=mesh['pop'=8,'unit'=16] {'unit'}, use_global_device_ids=true, to_apply=%region_9.10 | all-reduce | flops 16384 | bytes 65536 | tf_op jit(solution)/shard_map/psum | solution.py:112
  542.8 3.4 all-to-all-start.6
  546.3 5.5 all-to-all-done.6
  552.0 1.7 convolution_bitcast_fusion.10
  553.8 1.7 convolution_bitcast_fusion.11
  556.3 2.7 fusion.20
  562.2 3.4 all-to-all-start.8
  566.0 6.3 all-to-all-done.8
  575.1 69.6 %psum.69 = bf16[128,128]{0,1:T(8,128)(2,1)S(1)} all-reduce(bf16[128,128]{0,1:T(8,128)(2,1)S(1)} %fusion.202), channel_id=1, replica_groups=mesh['pop'=8,'unit'=16] {'unit'}, use_global_device_ids=true, to_apply=%region_12.13 | all-reduce | flops 16384 | bytes 65536 | tf_op jit(solution)/shard_map/psum | solution.py:112
  645.8 3.4 all-to-all-start.9
  649.2 5.9 fusion.32
  655.3 1.7 convolution_bitcast_fusion.4
  657.0 1.7 convolution_bitcast_fusion.5
  659.5 2.7 fusion.27
  665.1 4.7 all-to-all-start.11
  669.8 1.7 reshape.206
  671.5 5.1 all-to-all-done.11
  676.7 48.4 %reduce-scatter.11.cloned.1.call-done = bf16[256,128]{0,1:T(8,128)(2,1)} async-done(((bf16[4096,128]{0,1:T(8,128)(2,1)}), bf16[256,128]{0,1:T(8,128)(2,1)}) %reduce-scatter.11.cloned.1.call-update) | async-done | bytes 65552 | tf_op jit(solution)/shard_map/reduce_scatter | solution.py:104
  (232 shorter events, 59.6 us)
Async XLA Ops:
  7.2 88.0 %copy-start = (bf16[128,3,256]{2,0,1:T(8,128)(2,1)S(1)}, bf16[128,3,256]{2,0,1:T(8,128)(2,1)}, u32[]{:S(2)}) copy-start(bf16[128,3,256]{2,0,1:T(8,128)(2,1)} %param.14) | copy-start | bytes 589828
  11.7 11.2 %all-to-all-start.1 = ((bf16[256,4,96]{0,1,2:T(4,128)(2,1)}), bf16[256,4,96]{0,1,2:T(4,128)(2,1)S(1)}, u32[]{:S(2)}, u32[]{:S(2)}) async-start(bf16[256,4,96]{0,1,2:T(4,128)(2,1)} %copy.140), calls=%async_computation.2 | async-start | bytes 393216 | tf_op jit(solution)/shard_map/all_to_all | solution.py:125
  22.9 13.7 %all-to-all-start.4 = ((bf16[256,4,96]{0,1,2:T(4,128)(2,1)}), bf16[256,4,96]{0,1,2:T(4,128)(2,1)S(1)}, u32[]{:S(2)}, u32[]{:S(2)}) async-start(bf16[256,4,96]{0,1,2:T(4,128)(2,1)} %copy.159), calls=%async_computation.6 | async-start | bytes 393216 | tf_op jit(solution)/shard_map/all_to_all | solution.py:125
  36.6 0.7 copy-start.16
  37.3 19.5 %all-to-all-start.7 = ((bf16[256,4,96]{0,1,2:T(4,128)(2,1)}), bf16[256,4,96]{0,1,2:T(4,128)(2,1)S(1)}, u32[]{:S(2)}, u32[]{:S(2)}) async-start(bf16[256,4,96]{0,1,2:T(4,128)(2,1)} %copy.178), calls=%async_computation.10 | async-start | bytes 393216 | tf_op jit(solution)/shard_map/all_to_all | solution.py:125
  56.7 18.5 %all-to-all-start.10 = ((bf16[256,4,96]{0,1,2:T(4,128)(2,1)}), bf16[256,4,96]{0,1,2:T(4,128)(2,1)}, u32[]{:S(2)}, u32[]{:S(2)}) async-start(bf16[256,4,96]{0,1,2:T(4,128)(2,1)} %copy.197), calls=%async_computation.14 | async-start | bytes 393216 | tf_op jit(solution)/shard_map/all_to_all | solution.py:125
  61.6 215.3 %all-reduce.6.cloned.1.call-start = ((), (), s32[]{:S(2)}) async-start(), calls=%async_computation.21 | async-start | bytes 25165824 | tf_op jit(solution)/shard_map/psum | solution.py:36
  79.2 7.3 copy-start.5
  79.2 7.3 copy-start.6
  79.2 7.3 copy-start.7
  79.2 7.3 copy-start.8
  86.5 3.1 copy-start.9
  86.5 3.1 copy-start.10
  86.5 3.1 copy-start.11
  86.5 3.4 copy-start.12
  93.0 1.1 copy-start.18
  93.0 1.5 copy-start.17
  93.0 1.7 copy-start.40
  93.0 1.8 copy-start.19
  94.3 92.2 %copy-start.33 = (bf16[1,1,256,128]{2,3,1,0:T(8,128)(2,1)}, bf16[1,1,256,128]{2,3,1,0:T(8,128)(2,1)S(1)}, u32[]{:S(2)}) copy-start(bf16[1,1,256,128]{2,3,1,0:T(8,128)(2,1)S(1)} %copy.215) | copy-start | bytes 196612
  174.9 22.7 %all-to-all-start = ((bf16[128,4,96]{0,1,2:T(4,128)(2,1)}), bf16[128,4,96]{0,1,2:T(4,128)(2,1)S(1)}, u32[]{:S(2)}, u32[]{:S(2)}) async-start(bf16[128,4,96]{0,1,2:T(4,128)(2,1)} %copy.135), calls=%async_computation.1 | async-start | bytes 196608 | tf_op jit(solution)/shard_map/all_to_all | solution.py:126
  179.8 173.4 %reduce-scatter.5.cloned.1.call-start = ((), (), s32[]{:S(2)}) async-start(), calls=%async_computation.16 | async-start | bytes 1114112 | tf_op jit(solution)/shard_map/reduce_scatter | solution.py:104
  197.7 3.5 copy-start.1
  285.5 9.5 %copy-start.20 = (bf16[4,128,128]{2,1,0:T(8,128)(2,1)S(1)}, bf16[4,128,128]{2,1,0:T(8,128)(2,1)}, u32[]{:S(2)}) copy-start(bf16[4,128,128]{2,1,0:T(8,128)(2,1)} %param.11) | copy-start | bytes 393220
  285.5 67.7 %copy-start.34 = (bf16[1,1,256,128]{2,3,1,0:T(8,128)(2,1)S(1)}, bf16[1,1,256,128]{2,3,1,0:T(8,128)(2,1)}, u32[]{:S(2)}) copy-start(bf16[1,1,256,128]{2,3,1,0:T(8,128)(2,1)} %copy-done.33) | copy-start | bytes 196612
  285.5 67.6 %copy-start.36 = (bf16[256,128]{0,1:T(8,128)(2,1)S(1)}, bf16[256,128]{0,1:T(8,128)(2,1)}, u32[]{:S(2)}) copy-start(bf16[256,128]{0,1:T(8,128)(2,1)} %copy-done.35) | copy-start | bytes 196612
  287.7 66.6 %copy-start.26 = (bf16[1,1,256,128]{2,3,1,0:T(8,128)(2,1)S(1)}, bf16[1,1,256,128]{2,3,1,0:T(8,128)(2,1)}, u32[]{:S(2)}) copy-start(bf16[1,1,256,128]{2,3,1,0:T(8,128)(2,1)} %copy.228) | copy-start | bytes 196612
  287.7 66.6 %copy-start.30 = (bf16[1,1,256,128]{2,3,1,0:T(8,128)(2,1)S(1)}, bf16[1,1,256,128]{2,3,1,0:T(8,128)(2,1)}, u32[]{:S(2)}) copy-start(bf16[1,1,256,128]{2,3,1,0:T(8,128)(2,1)} %copy.229) | copy-start | bytes 196612
  287.7 66.6 %copy-start.31 = (bf16[1,1,256,128]{2,3,1,0:T(8,128)(2,1)S(1)}, bf16[1,1,256,128]{2,3,1,0:T(8,128)(2,1)}, u32[]{:S(2)}) copy-start(bf16[1,1,256,128]{2,3,1,0:T(8,128)(2,1)} %copy.230) | copy-start | bytes 196612
  287.7 66.6 %copy-start.32 = (bf16[1,256,128]{1,2,0:T(8,128)(2,1)S(1)}, bf16[1,256,128]{1,2,0:T(8,128)(2,1)}, u32[]{:S(2)}) copy-start(bf16[1,256,128]{1,2,0:T(8,128)(2,1)} %copy.231) | copy-start | bytes 196612
  290.7 11.1 %all-to-all-start.2 = ((bf16[256,4,96]{0,1,2:T(4,128)(2,1)}), bf16[256,4,96]{0,1,2:T(4,128)(2,1)S(1)}, u32[]{:S(2)}, u32[]{:S(2)}) async-start(bf16[256,4,96]{0,1,2:T(4,128)(2,1)} %copy.145), calls=%async_computation.3 | async-start | bytes 393216 | tf_op jit(solution)/shard_map/all_to_all | solution.py:129
  295.0 169.7 %reduce-scatter.7.cloned.1.call-start = ((), (), s32[]{:S(2)}) async-start(), calls=%async_computation.17 | async-start | bytes 1114112 | tf_op jit(solution)/shard_map/reduce_scatter | solution.py:104
  354.4 78.4 %copy-start.39 = (bf16[1,128,128]{1,2,0:T(8,128)(2,1)S(1)}, bf16[1,128,128]{1,2,0:T(8,128)(2,1)}, u32[]{:S(2)}) copy-start(bf16[1,128,128]{1,2,0:T(8,128)(2,1)} %copy.232) | copy-start | bytes 98308
  433.9 10.2 %all-to-all-start.3 = ((bf16[128,4,96]{0,1,2:T(4,128)(2,1)}), bf16[128,4,96]{0,1,2:T(4,128)(2,1)S(1)}, u32[]{:S(2)}, u32[]{:S(2)}) async-start(bf16[128,4,96]{0,1,2:T(4,128)(2,1)} %copy.154), calls=%async_computation.5 | async-start | bytes 196608 | tf_op jit(solution)/shard_map/all_to_all | solution.py:126
  444.1 3.6 copy-start.2
  446.0 2.5 copy-start.15
  448.1 3.1 slice-start
  448.5 3.1 slice-start.1
  453.0 12.7 %copy-start.22 = (bf16[1,1,256,128]{2,3,1,0:T(8,128)(2,1)S(1)}, bf16[1,1,256,128]{2,3,1,0:T(8,128)(2,1)}, u32[]{:S(2)}) copy-start(bf16[1,1,256,128]{2,3,1,0:T(8,128)(2,1)} %copy.241) | copy-start | bytes 196612
  453.0 12.7 %copy-start.27 = (bf16[1,1,256,128]{2,3,1,0:T(8,128)(2,1)S(1)}, bf16[1,1,256,128]{2,3,1,0:T(8,128)(2,1)}, u32[]{:S(2)}) copy-start(bf16[1,1,256,128]{2,3,1,0:T(8,128)(2,1)} %copy.242) | copy-start | bytes 196612
  453.1 12.7 %copy-start.28 = (bf16[1,1,256,128]{2,3,1,0:T(8,128)(2,1)S(1)}, bf16[1,1,256,128]{2,3,1,0:T(8,128)(2,1)}, u32[]{:S(2)}) copy-start(bf16[1,1,256,128]{2,3,1,0:T(8,128)(2,1)} %copy.243) | copy-start | bytes 196612
  453.1 12.7 %copy-start.29 = (bf16[1,256,128]{1,2,0:T(8,128)(2,1)S(1)}, bf16[1,256,128]{1,2,0:T(8,128)(2,1)}, u32[]{:S(2)}) copy-start(bf16[1,256,128]{1,2,0:T(8,128)(2,1)} %copy.244) | copy-start | bytes 196612
  454.4 10.2 %all-to-all-start.5 = ((bf16[256,4,96]{0,1,2:T(4,128)(2,1)}), bf16[256,4,96]{0,1,2:T(4,128)(2,1)S(1)}, u32[]{:S(2)}, u32[]{:S(2)}) async-start(bf16[256,4,96]{0,1,2:T(4,128)(2,1)} %copy.164), calls=%async_computation.7 | async-start | bytes 393216 | tf_op jit(solution)/shard_map/all_to_all | solution.py:129
  457.8 114.5 %reduce-scatter.9.cloned.1.call-start = ((), (), s32[]{:S(2)}) async-start(), calls=%async_computation.18 | async-start | bytes 1114112 | tf_op jit(solution)/shard_map/reduce_scatter | solution.py:104
  465.9 75.8 %copy-start.38 = (bf16[1,128,128]{1,2,0:T(8,128)(2,1)S(1)}, bf16[1,128,128]{1,2,0:T(8,128)(2,1)}, u32[]{:S(2)}) copy-start(bf16[1,128,128]{1,2,0:T(8,128)(2,1)} %copy.245) | copy-start | bytes 98308
  542.8 9.1 %all-to-all-start.6 = ((bf16[128,4,96]{0,1,2:T(4,128)(2,1)}), bf16[128,4,96]{0,1,2:T(4,128)(2,1)S(1)}, u32[]{:S(2)}, u32[]{:S(2)}) async-start(bf16[128,4,96]{0,1,2:T(4,128)(2,1)} %copy.173), calls=%async_computation.9 | async-start | bytes 196608 | tf_op jit(solution)/shard_map/all_to_all | solution.py:126
  551.9 3.6 copy-start.3
  553.7 2.5 copy-start.14
  555.9 3.1 slice-start.2
  556.3 3.1 slice-start.3
  560.8 12.7 %copy-start.21 = (bf16[1,1,256,128]{2,3,1,0:T(8,128)(2,1)S(1)}, bf16[1,1,256,128]{2,3,1,0:T(8,128)(2,1)}, u32[]{:S(2)}) copy-start(bf16[1,1,256,128]{2,3,1,0:T(8,128)(2,1)} %copy.254) | copy-start | bytes 196612
  560.8 12.7 %copy-start.23 = (bf16[1,1,256,128]{2,3,1,0:T(8,128)(2,1)S(1)}, bf16[1,1,256,128]{2,3,1,0:T(8,128)(2,1)}, u32[]{:S(2)}) copy-start(bf16[1,1,256,128]{2,3,1,0:T(8,128)(2,1)} %copy.255) | copy-start | bytes 196612
  560.8 12.7 %copy-start.24 = (bf16[1,1,256,128]{2,3,1,0:T(8,128)(2,1)S(1)}, bf16[1,1,256,128]{2,3,1,0:T(8,128)(2,1)}, u32[]{:S(2)}) copy-start(bf16[1,1,256,128]{2,3,1,0:T(8,128)(2,1)} %copy.256) | copy-start | bytes 196612
  560.8 12.7 %copy-start.25 = (bf16[1,256,128]{1,2,0:T(8,128)(2,1)S(1)}, bf16[1,256,128]{1,2,0:T(8,128)(2,1)}, u32[]{:S(2)}) copy-start(bf16[1,256,128]{1,2,0:T(8,128)(2,1)} %copy.257) | copy-start | bytes 196612
  561.3 83.4 %copy-start.37 = (bf16[1,128,128]{1,2,0:T(8,128)(2,1)S(1)}, bf16[1,128,128]{1,2,0:T(8,128)(2,1)}, u32[]{:S(2)}) copy-start(bf16[1,128,128]{1,2,0:T(8,128)(2,1)} %copy.258) | copy-start | bytes 98308
  562.2 10.2 %all-to-all-start.8 = ((bf16[256,4,96]{0,1,2:T(4,128)(2,1)}), bf16[256,4,96]{0,1,2:T(4,128)(2,1)S(1)}, u32[]{:S(2)}, u32[]{:S(2)}) async-start(bf16[256,4,96]{0,1,2:T(4,128)(2,1)} %copy.183), calls=%async_computation.11 | async-start | bytes 393216 | tf_op jit(solution)/shard_map/all_to_all | solution.py:129
  565.6 104.3 %all-reduce.4.cloned.1.call-start = ((), (), s32[]{:S(2)}) async-start(), calls=%async_computation.20 | async-start | bytes 393216 | tf_op jit(solution)/shard_map/psum | solution.py:140
  645.8 9.3 %all-to-all-start.9 = ((bf16[128,4,96]{0,1,2:T(4,128)(2,1)}), bf16[128,4,96]{0,1,2:T(4,128)(2,1)S(1)}, u32[]{:S(2)}, u32[]{:S(2)}) async-start(bf16[128,4,96]{0,1,2:T(4,128)(2,1)} %copy.192), calls=%async_computation.13 | async-start | bytes 196608 | tf_op jit(solution)/shard_map/all_to_all | solution.py:126
  649.1 75.9 %reduce-scatter.11.cloned.1.call-start = ((), (), s32[]{:S(2)}) async-start(), calls=%async_computation.19 | async-start | bytes 1114112 | tf_op jit(solution)/shard_map/reduce_scatter | solution.py:104
  655.1 3.7 copy-start.4
  657.0 2.5 copy-start.13
  658.8 3.5 slice-start.4
  659.5 2.8 slice-start.5
  665.1 11.5 %all-to-all-start.11 = ((bf16[256,4,96]{0,1,2:T(4,128)(2,1)}), bf16[256,4,96]{0,1,2:T(4,128)(2,1)S(1)}, u32[]{:S(2)}, u32[]{:S(2)}) async-start(bf16[256,4,96]{0,1,2:T(4,128)(2,1)} %copy.202), calls=%async_computation.15 | async-start | bytes 393216 | tf_op jit(solution)/shard_map/all_to_all | solution.py:129
  (1 other events, 0.6 us)
Sparse Core Ops, SparseCore 0:
  93.1 183.7 all-reduce.5
  280.4 72.6 reduce-scatter.4
  360.7 72.2 reduce-scatter.6
  472.2 67.5 reduce-scatter.8
  575.3 53.9 all-reduce.3
  655.2 69.7 reduce-scatter.10
where the time goes:
time: 742 us; the launch traced here: 734 us
  blocking collectives  290 us (39%)
  waiting for transfers between devices  209 us (28%)
  matrix products  114 us (15%)
  starting transfers between devices  51 us (7%)
  local copies, waits for them, and re-layouts  31.5 us (4%)
  other arithmetic  23.6 us (3%)
  between operations  15.5 us (2%)
    psum x4, blocking collectives, body(): lax.psum(jnp.dot(action_flat, flat_grads, preferred_element_type=jnp.floa...  290 us
    reduce_scatter x4, waiting for transfers between devices, body(): lax.psum_scatter(jnp.dot(recur_flat, flat_grads, preferred_element_type=j...  99.7 us
    psum x1, waiting for transfers between devices, hidden_slope(): lax.psum(partial_sum.astype(jnp.bfloat16), 'unit').astype(jnp.float32)  72.7 us
    dot_general x16, matrix products, hidden_slope(): jnp.dot(opp_first[member], received[:, member, :], preferred_element_type...  45 us
    all_to_all x4, waiting for transfers between devices, body(): lax.all_to_all(opponent_backward(slope, incoming, opp_first, opp_second),...  24.5 us
    dot_general x4, matrix products, body(): jnp.dot(recur_flat, flat_grads, preferred_element_type=jnp.float32)  23.8 us
    dot_general x16, matrix products, opponent_backward(): jnp.dot(opp_second[member].T, incoming[:, member, :], preferred_element_t...  19 us
    all_to_all x4, starting transfers between devices, body(): lax.all_to_all(pack_rows(states[step]), 'pop', split_axis=2, concat_axis=...  18 us
  transfers between devices with their start and end apart: 18, of which 10 were waited for; matrix products, arithmetic and copies ran while one was open for 17% of the time, Pallas kernels for 0%

commit v1 on v0

--- a/solution.py
+++ b/solution.py
@@ -109,11 +109,14 @@
             scatter_dimension=0,
             tiled=True,
         ).astype(jnp.float32)
-        action_grad = lax.psum(
-            jnp.dot(action_flat, flat_grads, preferred_element_type=jnp.float32).astype(
-                jnp.bfloat16
+        action_grad = jnp.sum(
+            lax.all_gather(
+                jnp.dot(action_flat, flat_grads, preferred_element_type=jnp.float32).astype(
+                    jnp.bfloat16
+                ),
+                "unit",
             ),
-            "unit",
+            axis=0,
         ).astype(jnp.float32)
         weight_grad = weight_grad + jnp.dot(
             actions[step], flat_grads.T, preferred_element_type=jnp.float32

time: 742 us -> 669 us (0.902)
  blocking collectives: 290 us -> 102 us
  waiting for transfers between devices: 209 us -> 320 us
    psum x4 -> x0, blocking collectives: 290 us -> none  [body(): lax.psum(jnp.dot(action_flat, flat_grads, preferred_element_type=jnp.floa...]
    all_gather x0 -> x4, blocking collectives: none -> 102 us  [body(): lax.all_gather(jnp.dot(action_flat, flat_grads, preferred_element_type=jn...]
    reduce_scatter x4, waiting for transfers between devices: 99.7 us -> 157 us  [body(): lax.psum_scatter(jnp.dot(recur_flat, flat_grads, preferred_element_type=j...]
    psum x1, waiting for transfers between devices: 72.7 us -> 123 us  [hidden_slope(): lax.psum(partial_sum.astype(jnp.bfloat16), 'unit').astype(jnp.float32)]
    psum x1, waiting for transfers between devices: 0.01 us -> 8.5 us  [body(): lax.psum(weight_grad.astype(jnp.bfloat16), 'pop').astype(jnp.float32)]
    unnamed x116 -> x120, local copies, waits for them, and re-layouts: 15.6 us -> 16.1 us
  transfers between devices with their start and end apart: 18 -> 18, of which waited for: 10 -> 12; matrix products, arithmetic and copies ran while one was open for 17% -> 19% of each run, Pallas kernels for 0% -> 0%
where the time goes in v1:
time: 669 us; the launch traced here: 661 us
  waiting for transfers between devices  320 us (48%)
  matrix products  114 us (17%)
  blocking collectives  102 us (15%)
  starting transfers between devices  53 us (8%)
  local copies, waits for them, and re-layouts  32 us (5%)
  other arithmetic  24.7 us (4%)
  between operations  15.6 us (2%)
    reduce_scatter x4, waiting for transfers between devices, body(): lax.psum_scatter(jnp.dot(recur_flat, flat_grads, preferred_element_type=j...  157 us
    psum x1, waiting for transfers between devices, hidden_slope(): lax.psum(partial_sum.astype(jnp.bfloat16), 'unit').astype(jnp.float32)  123 us
    all_gather x4, blocking collectives, body(): lax.all_gather(jnp.dot(action_flat, flat_grads, preferred_element_type=jn...  102 us
    dot_general x16, matrix products, hidden_slope(): jnp.dot(opp_first[member], received[:, member, :], preferred_element_type...  45 us
    dot_general x4, matrix products, body(): jnp.dot(recur_flat, flat_grads, preferred_element_type=jnp.float32)  24 us
    all_to_all x4, waiting for transfers between devices, body(): lax.all_to_all(opponent_backward(slope, incoming, opp_first, opp_second),...  19.3 us
    dot_general x16, matrix products, opponent_backward(): jnp.dot(opp_second[member].T, incoming[:, member, :], preferred_element_t...  19.1 us
    all_to_all x4, starting transfers between devices, body(): lax.all_to_all(pack_rows(states[step]), 'pop', split_axis=2, concat_axis=...  18 us
  transfers between devices with their start and end apart: 18, of which 12 were waited for; matrix products, arithmetic and copies ran while one was open for 19% of the time, Pallas kernels for 0%

profile of v1, /device:TPU:0, one launch (start us, length us, event | category | flops | bytes accessed | tf_op | source)
XLA Modules:
  0.0 661.1 jit_solution(7714859334204871525)
XLA Ops:
  11.7 4.4 all-to-all-start.1
  22.9 4.0 all-to-all-start.4
  27.1 2.4 fusion.36
  29.5 2.4 fusion.37
  31.9 2.4 fusion.38
  34.2 2.4 fusion.39
  37.3 4.8 all-to-all-start.7
  43.7 3.2 fusion.40
  47.0 3.3 fusion.41
  50.2 3.3 fusion.42
  53.5 3.3 fusion.43
  56.7 4.8 all-to-all-start.10
  62.2 3.2 fusion.44
  65.4 3.2 fusion.45
  68.7 3.3 fusion.46
  71.9 3.3 fusion.47
  76.8 2.4 fusion.48
  79.2 2.5 fusion.49
  81.7 2.4 fusion.50
  84.1 2.4 fusion.51
  86.5 3.1 pad_maximum_fusion
  90.0 3.0 pad_maximum_fusion.2
  95.2 28.9 %all-gather = bf16[2048,128]{0,1:T(8,128)(2,1)S(1)} all-gather(bf16[128,128]{0,1:T(8,128)(2,1)S(1)} %fusion.205), channel_id=2, replica_groups=mesh['pop'=8,'unit'=16] {'unit'}, dimensions={0}, use_global_device_ids=true | all-gather | bytes 557056 | tf_op jit(solution)/shard_map/all_gather | solution.py:113
  125.7 5.0 all-to-all-start
  131.3 6.4 fusion.35
  149.0 1.8 convolution_bitcast_fusion.16
  155.4 122.9 %all-reduce.6.cloned.1.call-done = (bf16[4096,384]{0,1:T(8,128)(2,1)}, bf16[4096,384]{0,1:T(8,128)(2,1)}, bf16[4096,384]{0,1:T(8,128)(2,1)}, bf16[4096,384]{0,1:T(8,128)(2,1)}) async-done(((bf16[4096,384]{0,1:T(8,128)(2,1)}, bf16[4096,384]{0,1:T(8,128)(2,1)}, bf16[4096,384]{0,1:T(8,128)(2,1)}, bf16[4096,384]{0,1:T(8,128)(2,1)}), (bf16[4096,384]{0,1:T(8,128)(2,1)}, bf16[4096,384]{0,1:T(8,128)(2,1)}, ...) | async-done | bytes 12582928 | tf_op jit(solution)/shard_map/psum | solution.py:36
  278.3 4.4 fusion.6
  282.7 2.1 fusion.163
  284.8 2.1 fusion.175
  286.9 2.1 fusion.187
  289.1 2.1 fusion.199
  292.1 4.3 all-to-all-start.2
  296.6 6.6 all-to-all-done.2
  303.2 51.3 %reduce-scatter.5.cloned.1.call-done = bf16[256,128]{0,1:T(8,128)(2,1)} async-done(((bf16[4096,128]{0,1:T(8,128)(2,1)}), bf16[256,128]{0,1:T(8,128)(2,1)}) %reduce-scatter.5.cloned.1.call-update) | async-done | bytes 65552 | tf_op jit(solution)/shard_map/reduce_scatter | solution.py:104
  355.9 5.9 fusion.34
  362.0 24.6 %all-gather.1 = bf16[2048,128]{0,1:T(8,128)(2,1)S(1)} all-gather(bf16[128,128]{0,1:T(8,128)(2,1)S(1)} %fusion.204), channel_id=3, replica_groups=mesh['pop'=8,'unit'=16] {'unit'}, dimensions={0}, use_global_device_ids=true | all-gather | bytes 557056 | tf_op jit(solution)/shard_map/all_gather | solution.py:113
  388.1 4.5 all-to-all-start.3
  392.8 5.6 all-to-all-done.3
  398.5 1.7 convolution_bitcast_fusion.12
  400.2 1.7 convolution_bitcast_fusion.13
  402.7 2.7 fusion.13
  408.7 3.4 all-to-all-start.5
  412.4 6.5 all-to-all-done.5
  418.9 15.9 %reduce-scatter.7.cloned.1.call-done = bf16[256,128]{0,1:T(8,128)(2,1)} async-done(((bf16[4096,128]{0,1:T(8,128)(2,1)}), bf16[256,128]{0,1:T(8,128)(2,1)}) %reduce-scatter.7.cloned.1.call-update) | async-done | bytes 65552 | tf_op jit(solution)/shard_map/reduce_scatter | solution.py:104
  436.0 5.9 fusion.33
  442.2 24.6 %all-gather.2 = bf16[2048,128]{0,1:T(8,128)(2,1)S(1)} all-gather(bf16[128,128]{0,1:T(8,128)(2,1)S(1)} %fusion.203), channel_id=4, replica_groups=mesh['pop'=8,'unit'=16] {'unit'}, dimensions={0}, use_global_device_ids=true | all-gather | bytes 557056 | tf_op jit(solution)/shard_map/all_gather | solution.py:113
  468.3 4.2 all-to-all-start.6
  472.7 5.6 all-to-all-done.6
  478.5 1.7 convolution_bitcast_fusion.10
  480.2 1.7 convolution_bitcast_fusion.11
  482.8 2.7 fusion.20
  488.7 3.5 all-to-all-start.8
  492.7 6.3 all-to-all-done.8
  499.0 15.8 %reduce-scatter.9.cloned.1.call-done = bf16[256,128]{0,1:T(8,128)(2,1)} async-done(((bf16[4096,128]{0,1:T(8,128)(2,1)}), bf16[256,128]{0,1:T(8,128)(2,1)}) %reduce-scatter.9.cloned.1.call-update) | async-done | bytes 65552 | tf_op jit(solution)/shard_map/reduce_scatter | solution.py:104
  517.6 24.1 %all-gather.3 = bf16[2048,128]{0,1:T(8,128)(2,1)S(1)} all-gather(bf16[128,128]{0,1:T(8,128)(2,1)S(1)} %fusion.202), channel_id=5, replica_groups=mesh['pop'=8,'unit'=16] {'unit'}, dimensions={0}, use_global_device_ids=true | all-gather | bytes 557056 | tf_op jit(solution)/shard_map/all_gather | solution.py:113
  543.1 4.2 all-to-all-start.9
  547.4 5.9 fusion.32
  553.5 1.7 convolution_bitcast_fusion.4
  555.2 1.7 convolution_bitcast_fusion.5
  557.8 2.7 fusion.27
  563.3 4.8 all-to-all-start.11
  568.1 8.5 %all-reduce.4.cloned.1.call-done = bf16[128,3,256]{2,0,1:T(8,128)(2,1)} async-done(((bf16[128,3,256]{2,0,1:T(8,128)(2,1)}), bf16[128,3,256]{2,0,1:T(8,128)(2,1)}) %all-reduce.4.cloned.1.call-update) | async-done | bytes 196624 | tf_op jit(solution)/shard_map/psum | solution.py:143
  578.3 73.9 %reduce-scatter.11.cloned.1.call-done = bf16[256,128]{0,1:T(8,128)(2,1)} async-done(((bf16[4096,128]{0,1:T(8,128)(2,1)}), bf16[256,128]{0,1:T(8,128)(2,1)}) %reduce-scatter.11.cloned.1.call-update) | async-done | bytes 65552 | tf_op jit(solution)/shard_map/reduce_scatter | solution.py:104
  (240 shorter events, 64.4 us)
Async XLA Ops:
  7.2 87.8 %copy-start = (bf16[128,3,256]{2,0,1:T(8,128)(2,1)S(1)}, bf16[128,3,256]{2,0,1:T(8,128)(2,1)}, u32[]{:S(2)}) copy-start(bf16[128,3,256]{2,0,1:T(8,128)(2,1)} %param.14) | copy-start | bytes 589828
  11.7 11.2 %all-to-all-start.1 = ((bf16[256,4,96]{0,1,2:T(4,128)(2,1)}), bf16[256,4,96]{0,1,2:T(4,128)(2,1)S(1)}, u32[]{:S(2)}, u32[]{:S(2)}) async-start(bf16[256,4,96]{0,1,2:T(4,128)(2,1)} %copy.140), calls=%async_computation.2 | async-start | bytes 393216 | tf_op jit(solution)/shard_map/all_to_all | solution.py:128
  22.9 13.7 %all-to-all-start.4 = ((bf16[256,4,96]{0,1,2:T(4,128)(2,1)}), bf16[256,4,96]{0,1,2:T(4,128)(2,1)S(1)}, u32[]{:S(2)}, u32[]{:S(2)}) async-start(bf16[256,4,96]{0,1,2:T(4,128)(2,1)} %copy.159), calls=%async_computation.6 | async-start | bytes 393216 | tf_op jit(solution)/shard_map/all_to_all | solution.py:128
  37.3 19.5 %all-to-all-start.7 = ((bf16[256,4,96]{0,1,2:T(4,128)(2,1)}), bf16[256,4,96]{0,1,2:T(4,128)(2,1)S(1)}, u32[]{:S(2)}, u32[]{:S(2)}) async-start(bf16[256,4,96]{0,1,2:T(4,128)(2,1)} %copy.178), calls=%async_computation.10 | async-start | bytes 393216 | tf_op jit(solution)/shard_map/all_to_all | solution.py:128
  56.7 18.5 %all-to-all-start.10 = ((bf16[256,4,96]{0,1,2:T(4,128)(2,1)}), bf16[256,4,96]{0,1,2:T(4,128)(2,1)}, u32[]{:S(2)}, u32[]{:S(2)}) async-start(bf16[256,4,96]{0,1,2:T(4,128)(2,1)} %copy.197), calls=%async_computation.14 | async-start | bytes 393216 | tf_op jit(solution)/shard_map/all_to_all | solution.py:128
  61.6 216.8 %all-reduce.6.cloned.1.call-start = ((), (), s32[]{:S(2)}) async-start(), calls=%async_computation.21 | async-start | bytes 25165824 | tf_op jit(solution)/shard_map/psum | solution.py:36
  79.2 7.3 %copy-start.5 = (bf16[4096,96]{0,1:T(8,128)(2,1)S(1)}, bf16[4096,96]{0,1:T(8,128)(2,1)}, u32[]{:S(2)}) copy-start(bf16[4096,96]{0,1:T(8,128)(2,1)} %fusion.40) | copy-start | bytes 2359300
  79.2 7.3 %copy-start.6 = (bf16[4096,96]{0,1:T(8,128)(2,1)S(1)}, bf16[4096,96]{0,1:T(8,128)(2,1)}, u32[]{:S(2)}) copy-start(bf16[4096,96]{0,1:T(8,128)(2,1)} %fusion.41) | copy-start | bytes 2359300
  79.2 7.3 %copy-start.7 = (bf16[4096,96]{0,1:T(8,128)(2,1)S(1)}, bf16[4096,96]{0,1:T(8,128)(2,1)}, u32[]{:S(2)}) copy-start(bf16[4096,96]{0,1:T(8,128)(2,1)} %fusion.42) | copy-start | bytes 2359300
  79.2 7.3 %copy-start.8 = (bf16[4096,96]{0,1:T(8,128)(2,1)S(1)}, bf16[4096,96]{0,1:T(8,128)(2,1)}, u32[]{:S(2)}) copy-start(bf16[4096,96]{0,1:T(8,128)(2,1)} %fusion.43) | copy-start | bytes 2359300
  86.5 3.1 copy-start.9
  86.5 3.1 copy-start.10
  86.5 3.1 copy-start.11
  86.5 3.4 copy-start.12
  93.0 1.1 copy-start.18
  93.0 1.5 copy-start.17
  93.0 1.7 copy-start.40
  94.1 30.1 %copy-start.19 = (bf16[4,128,128]{2,1,0:T(8,128)(2,1)S(1)}, bf16[4,128,128]{2,1,0:T(8,128)(2,1)}, u32[]{:S(2)}) copy-start(bf16[4,128,128]{2,1,0:T(8,128)(2,1)} %param.11) | copy-start | bytes 393220
  94.3 29.8 %copy-start.33 = (bf16[1,1,256,128]{2,3,1,0:T(8,128)(2,1)}, bf16[1,1,256,128]{2,3,1,0:T(8,128)(2,1)S(1)}, u32[]{:S(2)}) copy-start(bf16[1,1,256,128]{2,3,1,0:T(8,128)(2,1)S(1)} %copy.215) | copy-start | bytes 196612
  94.8 29.3 %copy-start.35 = (bf16[256,128]{0,1:T(8,128)(2,1)}, bf16[256,128]{0,1:T(8,128)(2,1)S(1)}, u32[]{:S(2)}) copy-start(bf16[256,128]{0,1:T(8,128)(2,1)S(1)} %copy.128) | copy-start | bytes 196612
  125.7 23.1 %all-to-all-start = ((bf16[128,4,96]{0,1,2:T(4,128)(2,1)}), bf16[128,4,96]{0,1,2:T(4,128)(2,1)S(1)}, u32[]{:S(2)}, u32[]{:S(2)}) async-start(bf16[128,4,96]{0,1,2:T(4,128)(2,1)} %copy.135), calls=%async_computation.1 | async-start | bytes 196608 | tf_op jit(solution)/shard_map/all_to_all | solution.py:129
  130.7 223.9 %reduce-scatter.5.cloned.1.call-start = ((), (), s32[]{:S(2)}) async-start(), calls=%async_computation.16 | async-start | bytes 1114112 | tf_op jit(solution)/shard_map/reduce_scatter | solution.py:104
  148.8 3.6 copy-start.1
  286.9 9.5 %copy-start.20 = (bf16[4,128,128]{2,1,0:T(8,128)(2,1)S(1)}, bf16[4,128,128]{2,1,0:T(8,128)(2,1)}, u32[]{:S(2)}) copy-start(bf16[4,128,128]{2,1,0:T(8,128)(2,1)} %param.11) | copy-start | bytes 393220
  286.9 67.7 %copy-start.34 = (bf16[1,1,256,128]{2,3,1,0:T(8,128)(2,1)S(1)}, bf16[1,1,256,128]{2,3,1,0:T(8,128)(2,1)}, u32[]{:S(2)}) copy-start(bf16[1,1,256,128]{2,3,1,0:T(8,128)(2,1)} %copy-done.33) | copy-start | bytes 196612
  286.9 67.7 %copy-start.36 = (bf16[256,128]{0,1:T(8,128)(2,1)S(1)}, bf16[256,128]{0,1:T(8,128)(2,1)}, u32[]{:S(2)}) copy-start(bf16[256,128]{0,1:T(8,128)(2,1)} %copy-done.35) | copy-start | bytes 196612
  289.1 66.6 %copy-start.26 = (bf16[1,1,256,128]{2,3,1,0:T(8,128)(2,1)S(1)}, bf16[1,1,256,128]{2,3,1,0:T(8,128)(2,1)}, u32[]{:S(2)}) copy-start(bf16[1,1,256,128]{2,3,1,0:T(8,128)(2,1)} %copy.228) | copy-start | bytes 196612
  289.1 66.6 %copy-start.30 = (bf16[1,1,256,128]{2,3,1,0:T(8,128)(2,1)S(1)}, bf16[1,1,256,128]{2,3,1,0:T(8,128)(2,1)}, u32[]{:S(2)}) copy-start(bf16[1,1,256,128]{2,3,1,0:T(8,128)(2,1)} %copy.229) | copy-start | bytes 196612
  289.1 66.6 %copy-start.31 = (bf16[1,1,256,128]{2,3,1,0:T(8,128)(2,1)S(1)}, bf16[1,1,256,128]{2,3,1,0:T(8,128)(2,1)}, u32[]{:S(2)}) copy-start(bf16[1,1,256,128]{2,3,1,0:T(8,128)(2,1)} %copy.230) | copy-start | bytes 196612
  289.1 66.6 %copy-start.32 = (bf16[1,256,128]{1,2,0:T(8,128)(2,1)S(1)}, bf16[1,256,128]{1,2,0:T(8,128)(2,1)}, u32[]{:S(2)}) copy-start(bf16[1,256,128]{1,2,0:T(8,128)(2,1)} %copy.231) | copy-start | bytes 196612
  292.1 11.1 %all-to-all-start.2 = ((bf16[256,4,96]{0,1,2:T(4,128)(2,1)}), bf16[256,4,96]{0,1,2:T(4,128)(2,1)S(1)}, u32[]{:S(2)}, u32[]{:S(2)}) async-start(bf16[256,4,96]{0,1,2:T(4,128)(2,1)} %copy.145), calls=%async_computation.3 | async-start | bytes 393216 | tf_op jit(solution)/shard_map/all_to_all | solution.py:132
  296.4 138.4 %reduce-scatter.7.cloned.1.call-start = ((), (), s32[]{:S(2)}) async-start(), calls=%async_computation.17 | async-start | bytes 1114112 | tf_op jit(solution)/shard_map/reduce_scatter | solution.py:104
  355.9 31.1 %copy-start.39 = (bf16[1,128,128]{1,2,0:T(8,128)(2,1)S(1)}, bf16[1,128,128]{1,2,0:T(8,128)(2,1)}, u32[]{:S(2)}) copy-start(bf16[1,128,128]{1,2,0:T(8,128)(2,1)} %copy.232) | copy-start | bytes 98308
  388.1 10.2 %all-to-all-start.3 = ((bf16[128,4,96]{0,1,2:T(4,128)(2,1)}), bf16[128,4,96]{0,1,2:T(4,128)(2,1)S(1)}, u32[]{:S(2)}, u32[]{:S(2)}) async-start(bf16[128,4,96]{0,1,2:T(4,128)(2,1)} %copy.154), calls=%async_computation.5 | async-start | bytes 196608 | tf_op jit(solution)/shard_map/all_to_all | solution.py:129
  398.3 3.6 copy-start.2
  400.2 2.5 copy-start.15
  402.3 3.1 slice-start
  402.7 3.2 slice-start.1
  407.3 28.5 %copy-start.22 = (bf16[1,1,256,128]{2,3,1,0:T(8,128)(2,1)S(1)}, bf16[1,1,256,128]{2,3,1,0:T(8,128)(2,1)}, u32[]{:S(2)}) copy-start(bf16[1,1,256,128]{2,3,1,0:T(8,128)(2,1)} %copy.241) | copy-start | bytes 196612
  407.3 28.5 %copy-start.27 = (bf16[1,1,256,128]{2,3,1,0:T(8,128)(2,1)S(1)}, bf16[1,1,256,128]{2,3,1,0:T(8,128)(2,1)}, u32[]{:S(2)}) copy-start(bf16[1,1,256,128]{2,3,1,0:T(8,128)(2,1)} %copy.242) | copy-start | bytes 196612
  407.3 28.5 %copy-start.28 = (bf16[1,1,256,128]{2,3,1,0:T(8,128)(2,1)S(1)}, bf16[1,1,256,128]{2,3,1,0:T(8,128)(2,1)}, u32[]{:S(2)}) copy-start(bf16[1,1,256,128]{2,3,1,0:T(8,128)(2,1)} %copy.243) | copy-start | bytes 196612
  407.3 28.5 %copy-start.29 = (bf16[1,256,128]{1,2,0:T(8,128)(2,1)S(1)}, bf16[1,256,128]{1,2,0:T(8,128)(2,1)}, u32[]{:S(2)}) copy-start(bf16[1,256,128]{1,2,0:T(8,128)(2,1)} %copy.244) | copy-start | bytes 196612
  408.7 10.2 %all-to-all-start.5 = ((bf16[256,4,96]{0,1,2:T(4,128)(2,1)}), bf16[256,4,96]{0,1,2:T(4,128)(2,1)S(1)}, u32[]{:S(2)}, u32[]{:S(2)}) async-start(bf16[256,4,96]{0,1,2:T(4,128)(2,1)} %copy.164), calls=%async_computation.7 | async-start | bytes 393216 | tf_op jit(solution)/shard_map/all_to_all | solution.py:132
  412.1 102.7 %reduce-scatter.9.cloned.1.call-start = ((), (), s32[]{:S(2)}) async-start(), calls=%async_computation.18 | async-start | bytes 1114112 | tf_op jit(solution)/shard_map/reduce_scatter | solution.py:104
  436.0 31.2 %copy-start.38 = (bf16[1,128,128]{1,2,0:T(8,128)(2,1)S(1)}, bf16[1,128,128]{1,2,0:T(8,128)(2,1)}, u32[]{:S(2)}) copy-start(bf16[1,128,128]{1,2,0:T(8,128)(2,1)} %copy.245) | copy-start | bytes 98308
  468.3 10.0 %all-to-all-start.6 = ((bf16[128,4,96]{0,1,2:T(4,128)(2,1)}), bf16[128,4,96]{0,1,2:T(4,128)(2,1)S(1)}, u32[]{:S(2)}, u32[]{:S(2)}) async-start(bf16[128,4,96]{0,1,2:T(4,128)(2,1)} %copy.173), calls=%async_computation.9 | async-start | bytes 196608 | tf_op jit(solution)/shard_map/all_to_all | solution.py:129
  478.3 3.6 copy-start.3
  480.2 2.5 copy-start.14
  482.3 3.1 slice-start.2
  482.7 3.2 slice-start.3
  487.3 28.6 %copy-start.21 = (bf16[1,1,256,128]{2,3,1,0:T(8,128)(2,1)S(1)}, bf16[1,1,256,128]{2,3,1,0:T(8,128)(2,1)}, u32[]{:S(2)}) copy-start(bf16[1,1,256,128]{2,3,1,0:T(8,128)(2,1)} %copy.254) | copy-start | bytes 196612
  487.3 28.6 %copy-start.23 = (bf16[1,1,256,128]{2,3,1,0:T(8,128)(2,1)S(1)}, bf16[1,1,256,128]{2,3,1,0:T(8,128)(2,1)}, u32[]{:S(2)}) copy-start(bf16[1,1,256,128]{2,3,1,0:T(8,128)(2,1)} %copy.255) | copy-start | bytes 196612
  487.3 28.6 %copy-start.24 = (bf16[1,1,256,128]{2,3,1,0:T(8,128)(2,1)S(1)}, bf16[1,1,256,128]{2,3,1,0:T(8,128)(2,1)}, u32[]{:S(2)}) copy-start(bf16[1,1,256,128]{2,3,1,0:T(8,128)(2,1)} %copy.256) | copy-start | bytes 196612
  487.4 28.6 %copy-start.25 = (bf16[1,256,128]{1,2,0:T(8,128)(2,1)S(1)}, bf16[1,256,128]{1,2,0:T(8,128)(2,1)}, u32[]{:S(2)}) copy-start(bf16[1,256,128]{1,2,0:T(8,128)(2,1)} %copy.257) | copy-start | bytes 196612
  488.7 53.3 %copy-start.37 = (bf16[1,128,128]{1,2,0:T(8,128)(2,1)S(1)}, bf16[1,128,128]{1,2,0:T(8,128)(2,1)}, u32[]{:S(2)}) copy-start(bf16[1,128,128]{1,2,0:T(8,128)(2,1)} %copy.258) | copy-start | bytes 98308
  488.7 10.3 %all-to-all-start.8 = ((bf16[256,4,96]{0,1,2:T(4,128)(2,1)}), bf16[256,4,96]{0,1,2:T(4,128)(2,1)S(1)}, u32[]{:S(2)}, u32[]{:S(2)}) async-start(bf16[256,4,96]{0,1,2:T(4,128)(2,1)} %copy.183), calls=%async_computation.11 | async-start | bytes 393216 | tf_op jit(solution)/shard_map/all_to_all | solution.py:132
  492.2 84.3 %all-reduce.4.cloned.1.call-start = ((), (), s32[]{:S(2)}) async-start(), calls=%async_computation.20 | async-start | bytes 393216 | tf_op jit(solution)/shard_map/psum | solution.py:143
  543.1 10.2 %all-to-all-start.9 = ((bf16[128,4,96]{0,1,2:T(4,128)(2,1)}), bf16[128,4,96]{0,1,2:T(4,128)(2,1)S(1)}, u32[]{:S(2)}, u32[]{:S(2)}) async-start(bf16[128,4,96]{0,1,2:T(4,128)(2,1)} %copy.192), calls=%async_computation.13 | async-start | bytes 196608 | tf_op jit(solution)/shard_map/all_to_all | solution.py:129
  547.4 104.9 %reduce-scatter.11.cloned.1.call-start = ((), (), s32[]{:S(2)}) async-start(), calls=%async_computation.19 | async-start | bytes 1114112 | tf_op jit(solution)/shard_map/reduce_scatter | solution.py:104
  553.3 3.7 copy-start.4
  555.2 2.5 copy-start.13
  557.0 3.5 slice-start.4
  557.7 2.8 slice-start.5
  563.3 15.0 %all-to-all-start.11 = ((bf16[256,4,96]{0,1,2:T(4,128)(2,1)}), bf16[256,4,96]{0,1,2:T(4,128)(2,1)S(1)}, u32[]{:S(2)}, u32[]{:S(2)}) async-start(bf16[256,4,96]{0,1,2:T(4,128)(2,1)} %copy.202), calls=%async_computation.15 | async-start | bytes 393216 | tf_op jit(solution)/shard_map/all_to_all | solution.py:132
  (1 other events, 0.7 us)
Sparse Core Ops, SparseCore 0:
  93.1 185.1 all-reduce.5
  281.8 72.6 reduce-scatter.4
  362.1 72.5 reduce-scatter.6
  442.3 72.4 reduce-scatter.8
  517.7 58.8 all-reduce.3
  580.0 72.2 reduce-scatter.10
